TPU v7x, 512 devices: a whole 4x8x8 slice. The times are simulated.
512 devices in a mesh: space: 32 (over z, x), vel: 16 (over y, core).
Axes of the slice: x: 4, y: 8, z: 8, core: 2. Of those that a mesh axis runs over, the one named last changes fastest.
Arguments:
- dist: bfloat16 [512, 64, 4096], P('space', None, 'vel'), may hold values from -6 to 6
- send_faces: int32 [32, 2, 16], P('space'), may hold values from 0 to 95
- send_count: int32 [32, 2], P('space'), may hold values from 1 to 16, as said below
- source_face: int32 [512, 6], P('space'), may hold values from 0 to 127, as said below
- subface: int32 [512, 6], P('space'), may hold values from 0 to 4
- alpha: float32 [4, 4096], replicated, may hold values from -1 to 1
- beta: float32 [5, 4096], replicated, may hold values from -1 to 1
Outputs:
- relaxed: bfloat16 [512, 64, 4096], P('space', None, 'vel')
Inputs may be any that keep to these rules, and one draw needn't show every extreme that they name: `source_face`: for each face of a block: below 96 a local face of the same block; from 96 the 16 slots of the previous block's block toward the next one, then the 16 slots of the next block's block toward the previous one. Every slot of these two blocks is read by exactly one face of the block. `send_count`: for each direction some block's padded trace block is full. `send_faces`: local face numbers, element times 6 plus face.
All inputs are finite; a program needn't handle non-finite values.
Results may differ from a plain program's by a relative error of at most 0.0057.
Values may be sent and summed in bfloat16 or wider, within the bound.
No kernel may reach another device: no remote copies, remote signals or barrier semaphores. Data moves between devices by JAX's collectives and lax.ppermute only.
A program may use at most 64 MiB of HBM per device.

v0:
```python
import jax
import jax.numpy as jnp
import numpy as np
from jax import lax
from jax.sharding import PartitionSpec as P

VSIDE = 16
VEL = 4096
courant = 0.1
lift_weight = 6.0
relax_step = 0.5
highest = lax.Precision.HIGHEST


def passed_along(block, axis, distance):
    devices = range(lax.axis_size(axis))
    route = [((i - distance) % len(devices), i) for i in devices]
    return lax.ppermute(block, axis, route)


def shortened(array):

    def short(part):
        return part.astype(jnp.bfloat16) if part.dtype == jnp.float32 else part

    return jax.tree.map(short, array)


def lobatto_points():
    return np.array([-1.0, -1.0 / np.sqrt(5.0), 1.0 / np.sqrt(5.0), 1.0])


def lagrange_table(targets):
    points = lobatto_points()
    result = np.ones((targets.shape[0], 4))
    for column in range(4):
        for second in range(4):
            if second != column:
                result[:, column] = (
                    result[:, column]
                    * (targets - points[second])
                    / (points[column] - points[second])
                )
    return result


def derivative_table():
    points = lobatto_points()
    result = np.zeros((4, 4))
    for row_at in range(4):
        for column in range(4):
            total = 0.0
            for skipped in range(4):
                if skipped != column:
                    factor = 1.0 / (points[column] - points[skipped])
                    for second in range(4):
                        if second != column and second != skipped:
                            factor = (
                                factor
                                * (points[row_at] - points[second])
                                / (points[column] - points[second])
                            )
                    total = total + factor
            result[row_at, column] = total
    return result


def cosine_table():
    index_list = np.arange(VSIDE)
    result = np.sqrt(2.0 / VSIDE) * np.cos(
        np.pi * (index_list[None, :] + 0.5) * index_list[:, None] / VSIDE
    )
    result[0] = result[0] / np.sqrt(2.0)
    return result


def static_tables():
    derivative = derivative_table()
    eye_four = np.eye(4)
    gradients = np.stack(
        [
            np.kron(np.kron(derivative, eye_four), eye_four),
            np.kron(np.kron(eye_four, derivative), eye_four),
            np.kron(np.kron(eye_four, eye_four), derivative),
        ]
    )
    selector = np.zeros((96, 64))
    for axis_at in range(3):
        for side_at in range(2):
            filled = 0
            for node_at in range(64):
                digits = (node_at // 16, node_at // 4 % 4, node_at % 4)
                if digits[axis_at] == 3 * side_at:
                    selector[(2 * axis_at + side_at) * 16 + filled, node_at] = 1.0
                    filled = filled + 1
    points = lobatto_points()
    halves = [lagrange_table((points - 1.0) / 2.0), lagrange_table((points + 1.0) / 2.0)]
    mortar = np.stack(
        [np.eye(16)]
        + [np.kron(halves[(which - 1) // 2], halves[(which - 1) % 2]) for which in range(1, 5)]
    )
    return (gradients, selector, mortar)


def velocity_components(first, count):
    index_list = first + jnp.arange(count)
    along = [index_list // (VSIDE * VSIDE), index_list // VSIDE % VSIDE, index_list % VSIDE]
    return jnp.stack([(entry.astype(jnp.float32) + 0.5) * (2.0 / VSIDE) - 1.0 for entry in along])


def collide_element(element, kernels, cosine, cosine_pair):
    width = element.shape[0]
    kernel_rows = kernels.shape[0]
    modes = (kernel_rows - 1) // 2
    values = element.astype(jnp.float32)
    cube = values.reshape(width, VSIDE, VSIDE * VSIDE)
    inner = jnp.einsum("nir,qr->niq", cube, cosine_pair, precision=highest)
    spectrum = jnp.einsum("ai,niq->naq", cosine, inner, precision=highest).reshape(width, 1, VEL)
    filtered = (spectrum * kernels[None]).reshape(width * kernel_rows, VSIDE, VSIDE * VSIDE)
    outer = jnp.einsum("ai,naq->niq", cosine, filtered, precision=highest)
    fields = jnp.einsum("niq,qr->nir", outer, cosine_pair, precision=highest).reshape(
        width, kernel_rows, VEL
    )
    gain = jnp.sum(fields[:, :modes] * fields[:, modes : 2 * modes], axis=1)
    loss = values * fields[:, 2 * modes]
    return (values + relax_step * (gain - loss)).astype(jnp.bfloat16)


def on_device(dist, send_faces, send_count, source_face, subface, alpha, beta):
    elements = dist.shape[0]
    vel_local = dist.shape[2]
    slots = send_faces.shape[2]
    gradients, selector, mortar = static_tables()
    grad_low = jnp.asarray(gradients, jnp.bfloat16)
    select_low = jnp.asarray(selector, jnp.bfloat16)
    select_full = jnp.asarray(selector, jnp.float32)
    mortar_low = jnp.asarray(mortar, jnp.bfloat16)
    speeds = velocity_components(lax.axis_index("vel") * vel_local, vel_local)
    rows = (
        jnp.einsum("tn,env->etv", select_low, dist, preferred_element_type=jnp.float32)
        .astype(jnp.bfloat16)
        .reshape(elements * 6, 16, vel_local)
    )
    picked = rows[send_faces[0].reshape(-1)].reshape(2, slots, 16, vel_local)
    live = jnp.arange(slots)[None, :] < send_count[0][:, None]
    outgoing = jnp.where(live[:, :, None, None], picked, jnp.zeros_like(picked))
    from_prev = passed_along(outgoing[1], "space", 1)
    from_next = passed_along(outgoing[0], "space", -1)
    drift = jnp.zeros(dist.shape, jnp.float32)
    for axis_at in range(3):
        drift = drift + speeds[axis_at] * jnp.einsum(
            "nm,emv->env", grad_low[axis_at], dist, preferred_element_type=jnp.float32
        )
    table = jnp.concatenate([rows, from_prev, from_next], axis=0)
    neighbour = table[source_face.reshape(-1)]
    projected = jnp.einsum(
        "ftu,fuv->ftv",
        mortar_low[subface.reshape(-1)],
        neighbour,
        preferred_element_type=jnp.float32,
    )
    inflow = jnp.minimum(
        jnp.stack([-speeds[0], speeds[0], -speeds[1], speeds[1], -speeds[2], speeds[2]]), 0.0
    )
    jump = (rows.astype(jnp.float32) - projected).reshape(elements, 6, 16, vel_local) * inflow[
        None, :, None, :
    ]
    lifted = jnp.einsum(
        "tn,etv->env", select_full, jump.reshape(elements, 96, vel_local), precision=highest
    )
    updated = (dist.astype(jnp.float32) - courant * drift + courant * lift_weight * lifted).astype(
        jnp.bfloat16
    )
    cosine_np = cosine_table()
    cosine = jnp.asarray(cosine_np, jnp.float32)
    cosine_pair = jnp.asarray(np.kron(cosine_np, cosine_np), jnp.float32)
    kernels = jnp.concatenate([alpha, beta], axis=0)

    def one_element(element):
        return collide_element(element, kernels, cosine, cosine_pair)

    mixed = lax.map(
        one_element, lax.all_to_all(updated, "vel", split_axis=1, concat_axis=2, tiled=True)
    )
    relaxed = lax.all_to_all(
        shortened(mixed), "vel", split_axis=2, concat_axis=1, tiled=True
    ).astype(mixed.dtype)
    return relaxed


def solution(mesh):
    return jax.shard_map(
        on_device,
        mesh=mesh,
        in_specs=(
            P("space", None, "vel"),
            P("space", None, None),
            P("space", None),
            P("space", None),
            P("space", None),
            P(),
            P(),
        ),
        out_specs=P("space", None, "vel"),
        check_vma=False,
    )
```

profile of v0, /device:TPU:1, one launch (start us, length us, event | category | flops | bytes accessed | tf_op | source)
XLA Modules:
  0.0 151.0 jit_solution(12709845251339062603)
XLA Ops:
  0.0 0.8 reshape_squeeze.3
  0.8 0.7 iota_compare_fusion
  1.6 1.4 convolution_convert_fusion
  3.7 4.0 %collective-permute-start = (bf16[16,16,256]{2,1,0:T(8,128)(2,1)S(1)}, bf16[16,16,256]{2,1,0:T(8,128)(2,1)S(1)}, u32[]{:S(2)}, u32[]{:S(2)}) collective-permute-start(bf16[16,16,256]{2,1,0:T(8,128)(2,1)S(1)} %get-tuple-element.63), channel_id=1, source_target_pairs={{496,0},{0,16},{16,32},{32,48},{48,64},{64,80},{80,96},{96,112},{1... | collective-permute-start | bytes 393224 | tf_op jit(solution)/shard_map/ppermute | solution.py:18
  7.7 11.7 %collective-permute-start.1 = (bf16[16,16,256]{2,1,0:T(8,128)(2,1)S(1)}, bf16[16,16,256]{2,1,0:T(8,128)(2,1)}, u32[]{:S(2)}, u32[]{:S(2)}) collective-permute-start(bf16[16,16,256]{2,1,0:T(8,128)(2,1)S(1)} %get-tuple-element.64), channel_id=1, source_target_pairs={{16,0},{32,16},{48,32},{64,48},{80,64},{96,80},{112,96},{128,112},... | collective-permute-start | bytes 393224 | tf_op jit(solution)/shard_map/ppermute | solution.py:18
  22.0 1.0 pad_maximum_fusion
  23.1 1.5 %gather_fusion.2 = bf16[96,16,256]{2,1,0:T(8,128)(2,1)} fusion(bf16[128,16,256]{2,1,0:T(8,128)(2,1)S(1)} %pad_maximum_fusion, s32[1024]{0:T(1024)S(1)} %pad_clamp_fusion), kind=kCustom, calls=%fused_computation.2 | custom fusion | bytes 1573248 | tf_op jit(solution)/shard_map/gather | solution.py:155
  24.6 1.5 convert_subtract_fusion
  26.9 1.2 fusion.13
  28.1 1.1 copy.25
  29.2 8.1 %all-to-all-start = ((bf16[16,64,256]{2,0,1:T(8,128)(2,1)}), bf16[16,64,256]{2,0,1:T(8,128)(2,1)S(1)}, u32[]{:S(2)}, u32[]{:S(2)}) async-start(bf16[16,64,256]{2,0,1:T(8,128)(2,1)} %copy.25), calls=%async_computation | async-start | bytes 1048576 | tf_op jit(solution)/shard_map/all_to_all | solution.py:183
  37.4 17.2 %all-to-all-done = bf16[16,64,256]{2,0,1:T(8,128)(2,1)S(1)} async-done(((bf16[16,64,256]{2,0,1:T(8,128)(2,1)}), bf16[16,64,256]{2,0,1:T(8,128)(2,1)S(1)}, u32[]{:S(2)}, u32[]{:S(2)}) %all-to-all-start) | async-done | bytes 524320 | tf_op jit(solution)/shard_map/all_to_all | solution.py:183
  54.7 54.8 %while.11 = (s32[]{:T(128)}, bf16[16,4,4096]{2,0,1:T(8,128)(2,1)S(1)}, bf16[16,4,4096]{2,0,1:T(8,128)(2,1)S(1)}, f32[9,4096]{1,0:T(8,128)S(1)}, s32[]{:T(128)}, ...) while((s32[]{:T(128)}, bf16[16,4,4096]{2,0,1:T(8,128)(2,1)S(1)}, ...), condition=%wide.region_2.3_spmd.clone, body=%wide.region_0.2_spmd.sunk.clone.sunk | while | flops 535134208 | bytes 7325801 | solution.py:182
  57.5 0.7 dynamic_update_slice.7
  74.6 0.7 dynamic_update_slice.7
  81.5 0.7 dynamic_update_slice.7
  84.9 0.7 dynamic_update_slice.7
  91.8 0.7 dynamic_update_slice.7
  109.6 4.6 %copy.27 = bf16[16,4,4096]{0,1,2:T(4,128)(2,1)} copy(bf16[16,4,4096]{2,0,1:T(8,128)(2,1)S(1)} %get-tuple-element.37) | data formatting | bytes 1048576 | tf_op jit(solution)/shard_map/while | solution.py:182
  114.2 5.7 %reshape.472 = bf16[16,2,8192]{2,1,0:T(2,128)(2,1)S(1)} reshape(bf16[4096,4,16]{2,1,0:T(4,128)(2,1)} %bitcast.110) | data formatting | bytes 1048576
  119.9 20.0 %all_to_all.36 = bf16[16,2,8192]{2,1,0:T(2,128)(2,1)S(1)} all-to-all(bf16[16,2,8192]{2,1,0:T(2,128)(2,1)S(1)} %reshape.472), channel_id=1, replica_groups=mesh['space'=32,'vel'=16] {'vel'}, dimensions={0} | all-to-all | bytes 1048576 | tf_op jit(solution)/shard_map/all_to_all | solution.py:185
  139.9 4.1 %reshape.473 = bf16[4096,4,16]{2,1,0:T(4,128)(2,1)} reshape(bf16[16,2,8192]{2,1,0:T(2,128)(2,1)S(1)} %all_to_all.36) | data formatting | bytes 1048576
  144.1 6.0 %copy.28 = bf16[16,16,4,256]{3,2,1,0:T(4,128)(2,1)S(1)} copy(bf16[16,16,4,256]{0,2,3,1:T(4,128)(2,1)} %bitcast.111) | data formatting | bytes 1048576 | tf_op jit(solution)/shard_map/all_to_all | solution.py:185
  150.1 0.9 all_to_all.33
  (242 shorter events, 54.0 us)
Async XLA Ops:
  0.0 19.9 %copy-start.9 = (bf16[64,64,1]{1,0,2:T(8,128)(2,1)S(1)}, bf16[64,64,1]{1,0,2:T(8,128)(2,1)}, u32[]{:S(2)}) copy-start(bf16[64,64,1]{1,0,2:T(8,128)(2,1)} %constant.122) | copy-start | bytes 24580
  0.0 20.0 %copy-start.1 = (bf16[16,64,256]{2,1,0:T(8,128)(2,1)S(1)}, bf16[16,64,256]{2,1,0:T(8,128)(2,1)}, u32[]{:S(2)}) copy-start(bf16[16,64,256]{2,1,0:T(8,128)(2,1)} %param.15) | copy-start | bytes 1572868
  0.0 19.5 %copy-start.10 = (s32[16,6]{0,1:T(8,128)S(1)}, s32[16,6]{0,1:T(8,128)}, u32[]{:S(2)}) copy-start(s32[16,6]{0,1:T(8,128)} %param.18) | copy-start | bytes 1156
  0.0 19.7 %copy-start.11 = (s32[16,6]{0,1:T(8,128)S(1)}, s32[16,6]{0,1:T(8,128)}, u32[]{:S(2)}) copy-start(s32[16,6]{0,1:T(8,128)} %param.19) | copy-start | bytes 1156
  3.0 17.3 %copy-start.8 = (bf16[64,64,1]{1,0,2:T(8,128)(2,1)S(1)}, bf16[64,64,1]{1,0,2:T(8,128)(2,1)}, u32[]{:S(2)}) copy-start(bf16[64,64,1]{1,0,2:T(8,128)(2,1)} %constant.123) | copy-start | bytes 24580
  3.7 18.3 %collective-permute-start = (bf16[16,16,256]{2,1,0:T(8,128)(2,1)S(1)}, bf16[16,16,256]{2,1,0:T(8,128)(2,1)S(1)}, u32[]{:S(2)}, u32[]{:S(2)}) collective-permute-start(bf16[16,16,256]{2,1,0:T(8,128)(2,1)S(1)} %get-tuple-element.63), channel_id=1, source_target_pairs={{496,0},{0,16},{16,32},{32,48},{48,64},{64,80},{80,96},{96,112},{1... | collective-permute-start | bytes 393224 | tf_op jit(solution)/shard_map/ppermute | solution.py:18
  7.7 14.3 %collective-permute-start.1 = (bf16[16,16,256]{2,1,0:T(8,128)(2,1)S(1)}, bf16[16,16,256]{2,1,0:T(8,128)(2,1)}, u32[]{:S(2)}, u32[]{:S(2)}) collective-permute-start(bf16[16,16,256]{2,1,0:T(8,128)(2,1)S(1)} %get-tuple-element.64), channel_id=1, source_target_pairs={{16,0},{32,16},{48,32},{64,48},{80,64},{96,80},{112,96},{128,112},... | collective-permute-start | bytes 393224 | tf_op jit(solution)/shard_map/ppermute | solution.py:18
  20.3 0.7 copy-start.7
  20.6 0.7 copy-start.2
  26.1 0.8 copy-start.6
  28.1 9.3 %copy-start.4 = (f32[5,4096]{1,0:T(8,128)S(1)}, f32[5,4096]{1,0:T(8,128)}, u32[]{:S(2)}) copy-start(f32[5,4096]{1,0:T(8,128)} %param.21) | copy-start | bytes 245764
  28.1 9.3 %copy-start.5 = (f32[4,4096]{1,0:T(4,128)S(1)}, f32[4,4096]{1,0:T(4,128)}, u32[]{:S(2)}) copy-start(f32[4,4096]{1,0:T(4,128)} %param.20) | copy-start | bytes 196612
  28.1 26.6 %copy-start = (f32[256,256,1]{1,0,2:T(8,128)S(1)}, f32[256,256,1]{1,0,2:T(8,128)}, u32[]{:S(2)}) copy-start(f32[256,256,1]{1,0,2:T(8,128)} %constant.232) | copy-start | bytes 786436
  28.1 26.6 %copy-start.3 = (f32[16,16,1]{1,0,2:T(8,128)S(1)}, f32[16,16,1]{1,0,2:T(8,128)}, u32[]{:S(2)}) copy-start(f32[16,16,1]{1,0,2:T(8,128)} %constant.233) | copy-start | bytes 3076
  29.2 25.5 %all-to-all-start = ((bf16[16,64,256]{2,0,1:T(8,128)(2,1)}), bf16[16,64,256]{2,0,1:T(8,128)(2,1)S(1)}, u32[]{:S(2)}, u32[]{:S(2)}) async-start(bf16[16,64,256]{2,0,1:T(8,128)(2,1)} %copy.25), calls=%async_computation | async-start | bytes 1048576 | tf_op jit(solution)/shard_map/all_to_all | solution.py:183
where the time goes:
time: 152 us; the launch traced here: 151 us
  local copies, waits for them, and re-layouts  45.7 us (30%)
  matrix products  33.2 us (22%)
  starting transfers between devices  23.8 us (16%)
  blocking collectives  20 us (13%)
  waiting for transfers between devices  17.3 us (11%)
  other arithmetic  9.18 us (6%)
  loops' own time  1.55 us (1%)
    all_to_all x1, blocking collectives, on_device(): lax.all_to_all(shortened(mixed), 'vel', split_axis=2, concat_axis=1, tile...  20 us
    all_to_all x1, waiting for transfers between devices, on_device(): lax.all_to_all(updated, 'vel', split_axis=1, concat_axis=2, tiled=True)  17.2 us
    ppermute x2, starting transfers between devices, passed_along(): return lax.ppermute(block, axis, route)  15.6 us
    unnamed x28, local copies, waits for them, and re-layouts  11.1 us
    dynamic_update_slice x16, local copies, waits for them, and re-layouts, on_device(): lax.map(one_element, lax.all_to_all(updated, 'vel', split_axis=1, concat_...  10.7 us
    dot_general x16, matrix products, collide_element(): outer = jnp.einsum('ai,naq->niq', cosine, filtered, precision=highest)  10.6 us
    dot_general x16, matrix products, collide_element(): jnp.einsum('niq,qr->nir', outer, cosine_pair, precision=highest)  10.1 us
    all_to_all x1, starting transfers between devices, on_device(): lax.all_to_all(updated, 'vel', split_axis=1, concat_axis=2, tiled=True)  8.15 us
  transfers between devices with their start and end apart: 3, of which 1 were waited for; matrix products, arithmetic and copies ran while one was open for 1% of the time, Pallas kernels for 0%

commit v1 on v0

--- a/solution.py
+++ b/solution.py
@@ -182,8 +182,11 @@
     mixed = lax.map(
         one_element, lax.all_to_all(updated, "vel", split_axis=1, concat_axis=2, tiled=True)
     )
-    relaxed = lax.all_to_all(
-        shortened(mixed), "vel", split_axis=2, concat_axis=1, tiled=True
+    relaxed = jnp.concatenate(
+        lax.all_to_all(
+            jnp.stack(jnp.split(shortened(mixed), lax.axis_size("vel"), axis=2)), "vel", 0, 0
+        ),
+        axis=1,
     ).astype(mixed.dtype)
     return relaxed
 

time: 152 us -> 133 us (0.88)
  local copies, waits for them, and re-layouts: 45.7 us -> 26.7 us
    unnamed x28 -> x45, local copies, waits for them, and re-layouts: 11.1 us -> 2.01 us
    all_to_all x2 -> x0, local copies, waits for them, and re-layouts: 6.95 us -> none  [on_device(): lax.all_to_all(shortened(mixed), 'vel', split_axis=2, concat_axis=1, tile...]
    while x17 -> x16, local copies, waits for them, and re-layouts: 5.33 us -> 0.73 us  [the longest x1 4.6 us: on_device(): lax.map(one_element, lax.all_to_all(updated, 'vel', split_axis=1, concat_...]
  transfers between devices with their start and end apart: 3 -> 3, of which waited for: 1 -> 1; matrix products, arithmetic and copies ran while one was open for 1% -> 2% of each run, Pallas kernels for 0% -> 0%
where the time goes in v1:
time: 133 us; the launch traced here: 132 us
  matrix products  33.3 us (25%)
  local copies, waits for them, and re-layouts  26.7 us (20%)
  starting transfers between devices  23.7 us (18%)
  blocking collectives  20 us (15%)
  waiting for transfers between devices  17.3 us (13%)
  other arithmetic  9.46 us (7%)
  loops' own time  1.42 us (1%)
    all_to_all x1, blocking collectives, on_device(): lax.all_to_all(jnp.stack(jnp.split(shortened(mixed), lax.axis_size('vel')...  20 us
    all_to_all x1, waiting for transfers between devices, on_device(): lax.all_to_all(updated, 'vel', split_axis=1, concat_axis=2, tiled=True)  17.2 us
    ppermute x2, starting transfers between devices, passed_along(): return lax.ppermute(block, axis, route)  15.6 us
    dynamic_update_slice x16, local copies, waits for them, and re-layouts, on_device(): lax.map(one_element, lax.all_to_all(updated, 'vel', split_axis=1, concat_...  10.7 us
    dot_general x16, matrix products, collide_element(): outer = jnp.einsum('ai,naq->niq', cosine, filtered, precision=highest)  10.6 us
    dot_general x16, matrix products, collide_element(): jnp.einsum('niq,qr->nir', outer, cosine_pair, precision=highest)  10.1 us
    all_to_all x1, starting transfers between devices, on_device(): lax.all_to_all(updated, 'vel', split_axis=1, concat_axis=2, tiled=True)  8.08 us
    dot_general x16, matrix products, collide_element(): inner = jnp.einsum('nir,qr->niq', cube, cosine_pair, precision=highest)  4.44 us
  transfers between devices with their start and end apart: 3, of which 1 were waited for; matrix products, arithmetic and copies ran while one was open for 2% of the time, Pallas kernels for 0%

profile of v1, /device:TPU:1, one launch (start us, length us, event | category | flops | bytes accessed | tf_op | source)
XLA Modules:
  0.0 132.3 jit_solution(8693689604470559746)
XLA Ops:
  0.0 0.8 reshape_squeeze.3
  0.8 0.7 iota_compare_fusion
  1.5 1.5 %convolution_convert_fusion = bf16[96,16,256]{2,0,1:T(8,128)(2,1)S(1)} fusion(bf16[96,64,1]{0,1,2:T(8,128)(2,1)} %constant.125, bf16[16,64,256]{2,1,0:T(8,128)(2,1)} %param.15), kind=kOutput, calls=%fused_computation.18 | convolution fusion | flops 50724864 | bytes 1323008 | tf_op jit(solution)/shard_map/tn,env->etv/dot_general | solution.py:140
  3.8 3.9 %collective-permute-start = (bf16[16,16,256]{2,1,0:T(8,128)(2,1)S(1)}, bf16[16,16,256]{2,1,0:T(8,128)(2,1)S(1)}, u32[]{:S(2)}, u32[]{:S(2)}) collective-permute-start(bf16[16,16,256]{2,1,0:T(8,128)(2,1)S(1)} %get-tuple-element.63), channel_id=1, source_target_pairs={{496,0},{0,16},{16,32},{32,48},{48,64},{64,80},{80,96},{96,112},{1... | collective-permute-start | bytes 393224 | tf_op jit(solution)/shard_map/ppermute | solution.py:18
  7.7 11.7 %collective-permute-start.1 = (bf16[16,16,256]{2,1,0:T(8,128)(2,1)S(1)}, bf16[16,16,256]{2,1,0:T(8,128)(2,1)}, u32[]{:S(2)}, u32[]{:S(2)}) collective-permute-start(bf16[16,16,256]{2,1,0:T(8,128)(2,1)S(1)} %get-tuple-element.64), channel_id=1, source_target_pairs={{16,0},{32,16},{48,32},{64,48},{80,64},{96,80},{112,96},{128,112},... | collective-permute-start | bytes 393224 | tf_op jit(solution)/shard_map/ppermute | solution.py:18
  19.9 1.4 %gather_fusion = bf16[96,16,16]{2,1,0:T(8,128)(2,1)} fusion(bf16[5,16,16]{2,1,0:T(8,128)(2,1)S(1)} %copy-done.2, s32[1024]{0:T(1024)S(1)} %get-tuple-element.74), kind=kCustom, calls=%fused_computation | custom fusion | bytes 98688 | tf_op jit(solution)/shard_map/gather | solution.py:158
  23.4 1.1 pad_maximum_fusion
  24.5 1.5 %gather_fusion.2 = bf16[96,16,256]{2,1,0:T(8,128)(2,1)} fusion(bf16[128,16,256]{2,1,0:T(8,128)(2,1)S(1)} %pad_maximum_fusion, s32[1024]{0:T(1024)S(1)} %get-tuple-element.73), kind=kCustom, calls=%fused_computation.2 | custom fusion | bytes 1573248 | tf_op jit(solution)/shard_map/gather | solution.py:155
  26.0 1.5 %convert_subtract_fusion = f32[96,16,256]{2,1,0:T(8,128)S(1)} fusion(bf16[96,16,256]{2,1,0:T(8,128)(2,1)S(1)} %bitcast.142, bf16[96,16,16]{2,1,0:T(8,128)(2,1)S(1)} %copy-done.3, bf16[96,16,256]{2,1,0:T(8,128)(2,1)} %gather_fusion.2), kind=kOutput, calls=%fused_computation.17 | convolution fusion | flops 13369344 | bytes 3194880 | tf_op jit(solution)/shard_map/ftu,fuv->ftv/dot_general | solution.py:156
  28.3 1.3 fusion.13
  29.6 1.1 copy.25
  30.7 8.1 %all-to-all-start = ((bf16[16,64,256]{2,0,1:T(8,128)(2,1)}), bf16[16,64,256]{2,0,1:T(8,128)(2,1)S(1)}, u32[]{:S(2)}, u32[]{:S(2)}) async-start(bf16[16,64,256]{2,0,1:T(8,128)(2,1)} %copy.25), calls=%async_computation | async-start | bytes 1048576 | tf_op jit(solution)/shard_map/all_to_all | solution.py:183
  38.8 17.2 %all-to-all-done = bf16[16,64,256]{2,0,1:T(8,128)(2,1)S(1)} async-done(((bf16[16,64,256]{2,0,1:T(8,128)(2,1)}), bf16[16,64,256]{2,0,1:T(8,128)(2,1)S(1)}, u32[]{:S(2)}, u32[]{:S(2)}) %all-to-all-start) | async-done | bytes 524320 | tf_op jit(solution)/shard_map/all_to_all | solution.py:183
  56.1 55.0 %while.11 = (s32[]{:T(128)}, bf16[16,4,4096]{2,0,1:T(8,128)(2,1)S(1)}, bf16[16,4,4096]{2,0,1:T(8,128)(2,1)S(1)}, f32[9,4096]{1,0:T(8,128)S(1)}, s32[]{:T(128)}, ...) while((s32[]{:T(128)}, bf16[16,4,4096]{2,0,1:T(8,128)(2,1)S(1)}, ...), condition=%wide.region_2.3_spmd.clone, body=%wide.region_0.2_spmd.sunk.clone.sunk | while | flops 535134208 | bytes 7325793 | solution.py:182
  58.9 0.7 dynamic_update_slice.7
  62.3 0.7 dynamic_update_slice.7
  65.7 0.7 dynamic_update_slice.7
  69.2 0.7 dynamic_update_slice.7
  72.6 0.7 dynamic_update_slice.7
  82.9 0.7 dynamic_update_slice.7
  96.7 0.7 dynamic_update_slice.7
  110.4 0.7 dynamic_update_slice.7
  111.3 20.0 %all_to_all.23 = bf16[16,16,4,256]{3,1,2,0:T(8,128)(2,1)S(1)} all-to-all(bf16[16,16,4,256]{3,1,2,0:T(8,128)(2,1)S(1)} %constant_dynamic-update-slice_fusion), channel_id=1, replica_groups=mesh['space'=32,'vel'=16] {'vel'}, dimensions={0} | all-to-all | bytes 1048576 | tf_op jit(solution)/shard_map/all_to_all | solution.py:186
  131.4 1.0 copy.29
  (257 shorter events, 52.3 us)
Async XLA Ops:
  0.0 19.9 %copy-start.2 = (bf16[5,16,16]{2,1,0:T(8,128)(2,1)S(1)}, bf16[5,16,16]{2,1,0:T(8,128)(2,1)}, u32[]{:S(2)}) copy-start(bf16[5,16,16]{2,1,0:T(8,128)(2,1)} %constant.108.clone) | copy-start | bytes 7684
  0.0 19.5 %copy-start.12 = (s32[16,6]{0,1:T(8,128)S(1)}, s32[16,6]{0,1:T(8,128)}, u32[]{:S(2)}) copy-start(s32[16,6]{0,1:T(8,128)} %param.19) | copy-start | bytes 1156
  0.0 19.7 %copy-start.13 = (s32[16,6]{0,1:T(8,128)S(1)}, s32[16,6]{0,1:T(8,128)}, u32[]{:S(2)}) copy-start(s32[16,6]{0,1:T(8,128)} %param.18) | copy-start | bytes 1156
  1.5 19.8 %copy-start.1 = (bf16[16,64,256]{2,1,0:T(8,128)(2,1)S(1)}, bf16[16,64,256]{2,1,0:T(8,128)(2,1)}, u32[]{:S(2)}) copy-start(bf16[16,64,256]{2,1,0:T(8,128)(2,1)} %param.15) | copy-start | bytes 1572868
  1.5 19.8 %copy-start.11 = (bf16[64,64,1]{1,0,2:T(8,128)(2,1)S(1)}, bf16[64,64,1]{1,0,2:T(8,128)(2,1)}, u32[]{:S(2)}) copy-start(bf16[64,64,1]{1,0,2:T(8,128)(2,1)} %constant.122) | copy-start | bytes 24580
  3.7 17.9 %copy-start.10 = (bf16[64,64,1]{1,0,2:T(8,128)(2,1)S(1)}, bf16[64,64,1]{1,0,2:T(8,128)(2,1)}, u32[]{:S(2)}) copy-start(bf16[64,64,1]{1,0,2:T(8,128)(2,1)} %constant.123) | copy-start | bytes 24580
  3.8 18.9 %collective-permute-start = (bf16[16,16,256]{2,1,0:T(8,128)(2,1)S(1)}, bf16[16,16,256]{2,1,0:T(8,128)(2,1)S(1)}, u32[]{:S(2)}, u32[]{:S(2)}) collective-permute-start(bf16[16,16,256]{2,1,0:T(8,128)(2,1)S(1)} %get-tuple-element.63), channel_id=1, source_target_pairs={{496,0},{0,16},{16,32},{32,48},{48,64},{64,80},{80,96},{96,112},{1... | collective-permute-start | bytes 393224 | tf_op jit(solution)/shard_map/ppermute | solution.py:18
  7.7 15.7 %collective-permute-start.1 = (bf16[16,16,256]{2,1,0:T(8,128)(2,1)S(1)}, bf16[16,16,256]{2,1,0:T(8,128)(2,1)}, u32[]{:S(2)}, u32[]{:S(2)}) collective-permute-start(bf16[16,16,256]{2,1,0:T(8,128)(2,1)S(1)} %get-tuple-element.64), channel_id=1, source_target_pairs={{16,0},{32,16},{48,32},{64,48},{80,64},{96,80},{112,96},{128,112},... | collective-permute-start | bytes 393224 | tf_op jit(solution)/shard_map/ppermute | solution.py:18
  21.6 0.7 copy-start.9
  22.7 3.3 %copy-start.3 = (bf16[96,16,16]{2,1,0:T(8,128)(2,1)S(1)}, bf16[96,16,16]{2,1,0:T(8,128)(2,1)}, u32[]{:S(2)}) copy-start(bf16[96,16,16]{2,1,0:T(8,128)(2,1)} %gather_fusion) | copy-start | bytes 147460
  22.7 0.6 copy-start.6
  27.5 0.8 copy-start.8
  29.5 9.2 %copy-start.5 = (f32[5,4096]{1,0:T(8,128)S(1)}, f32[5,4096]{1,0:T(8,128)}, u32[]{:S(2)}) copy-start(f32[5,4096]{1,0:T(8,128)} %param.21) | copy-start | bytes 245764
  29.5 9.2 %copy-start.7 = (f32[4,4096]{1,0:T(4,128)S(1)}, f32[4,4096]{1,0:T(4,128)}, u32[]{:S(2)}) copy-start(f32[4,4096]{1,0:T(4,128)} %param.20) | copy-start | bytes 196612
  29.6 26.6 %copy-start = (f32[256,256,1]{1,0,2:T(8,128)S(1)}, f32[256,256,1]{1,0,2:T(8,128)}, u32[]{:S(2)}) copy-start(f32[256,256,1]{1,0,2:T(8,128)} %constant.278) | copy-start | bytes 786436
  29.6 26.5 %copy-start.4 = (f32[16,16,1]{1,0,2:T(8,128)S(1)}, f32[16,16,1]{1,0,2:T(8,128)}, u32[]{:S(2)}) copy-start(f32[16,16,1]{1,0,2:T(8,128)} %constant.279) | copy-start | bytes 3076
  30.7 25.4 %all-to-all-start = ((bf16[16,64,256]{2,0,1:T(8,128)(2,1)}), bf16[16,64,256]{2,0,1:T(8,128)(2,1)S(1)}, u32[]{:S(2)}, u32[]{:S(2)}) async-start(bf16[16,64,256]{2,0,1:T(8,128)(2,1)} %copy.25), calls=%async_computation | async-start | bytes 1048576 | tf_op jit(solution)/shard_map/all_to_all | solution.py:183
